TPU v7x, 128 devices: a whole 4x4x4 slice. The times are simulated.
128 devices in a mesh: seq: 16 (over y, z), batch: 8 (over x, core).
Axes of the slice: x: 4, y: 4, z: 4, core: 2. Of those that a mesh axis runs over, the one named last changes fastest.
Arguments:
- inputs: bfloat16 [8, 16384, 2048], P('batch', 'seq'), may hold values from -6 to 6
- input_map: bfloat16 [8, 16384, 128], P('batch', 'seq'), may hold values from -0.5 to 0.5
- output_map: bfloat16 [8, 16384, 128], P('batch', 'seq'), may hold values from -0.5 to 0.5
- step_raw: float32 [8, 32, 16384], P('batch', None, 'seq'), may hold values from -4.5 to 4.5
- step_bias: float32 [32], replicated, may hold values from -2 to 0
- decay_rate: float32 [32], replicated, may hold values from 1.5258789e-05 to 0.05
- skip_gain: float32 [32], replicated, may hold values from 0.5 to 1.5
- cotangent: bfloat16 [8, 16384, 2048], P('batch', 'seq'), may hold values from -6 to 6
Outputs:
- grad_inputs: bfloat16 [8, 16384, 2048], P('batch', 'seq')
- grad_input_map: float32 [8, 16384, 128], P('batch', 'seq')
- grad_output_map: float32 [8, 16384, 128], P('batch', 'seq')
- grad_step_raw: float32 [8, 32, 16384], P('batch', None, 'seq')
- grad_params: float32 [2, 32], replicated
- grad_decay_rate: float32 [32], replicated
All inputs are finite; a program needn't handle non-finite values.
Results may differ from a plain program's by a relative error of at most 0.034.
Values sent between devices are 32-bit elements; how exact they have to be, the bound alone decides.
A program may use at most 192 MiB of HBM per device.

v0:
```python
import math
import jax
import jax.numpy as jnp
from jax import lax
from jax.sharding import PartitionSpec as P

GROUP = 256


def entering(array, axis, combine, identity, reverse):
    length, mine = (lax.axis_size(axis), lax.axis_index(axis))
    everything = jax.tree.map(lambda part: lax.all_gather(part, axis), array)
    start = jax.tree.map(
        lambda part, zero: jnp.broadcast_to(jnp.asarray(zero, part.dtype), part.shape),
        array,
        identity,
    )

    def lap(k, before):
        at = length - 1 - k if reverse else k
        reached = at > mine if reverse else at < mine
        new = combine(before, jax.tree.map(lambda part: part[at], everything))
        return jax.tree.map(lambda a, b: jnp.where(reached, a, b), new, before)

    return lax.fori_loop(0, length, lap, start)


def block_step(state, items, skip_gain):
    xc, bc, cc, stepc, logc = items
    width = xc.shape[0]
    cum = jnp.cumsum(logc, axis=1)
    rows = lax.broadcasted_iota(jnp.int32, (width, width), 0)
    cols = lax.broadcasted_iota(jnp.int32, (width, width), 1)
    lower = cols <= rows
    gap = jnp.where(lower[None], cum[:, :, None] - cum[:, None, :], -1e30)
    decay = jnp.exp(gap)
    scores = jnp.einsum("tn,sn->ts", cc, bc, preferred_element_type=jnp.float32)
    weights = (scores[None] * decay * stepc[:, None, :]).astype(jnp.bfloat16)
    inner = jnp.einsum("hts,shp->thp", weights, xc, preferred_element_type=jnp.float32)
    carried = (
        jnp.einsum(
            "tn,hpn->thp", cc, state.astype(jnp.bfloat16), preferred_element_type=jnp.float32
        )
        * jnp.exp(cum).T[:, :, None]
    )
    output = inner + carried + skip_gain[None, :, None] * xc.astype(jnp.float32)
    tail = jnp.exp(cum[:, -1:] - cum) * stepc
    scaled = (xc.astype(jnp.float32) * tail.T[:, :, None]).astype(jnp.bfloat16)
    fresh = jnp.einsum("shp,sn->hpn", scaled, bc, preferred_element_type=jnp.float32)
    new_state = jnp.exp(cum[:, -1])[:, None, None] * state + fresh
    return (new_state, output.astype(jnp.bfloat16))


def scan_forward(xb, bb, cb, raw, step_bias, decay_rate, skip_gain, start_state):
    length, heads, head_size = xb.shape
    states = bb.shape[1]
    blocks = length // GROUP
    step = jax.nn.softplus(raw + step_bias[:, None])
    logd = -decay_rate[:, None] * step
    xs = xb.reshape(blocks, GROUP, heads, head_size)
    bs = bb.reshape(blocks, GROUP, states)
    cs = cb.reshape(blocks, GROUP, states)
    steps = step.reshape(heads, blocks, GROUP).transpose(1, 0, 2)
    logs = logd.reshape(heads, blocks, GROUP).transpose(1, 0, 2)
    body_fn = jax.checkpoint(lambda s, it: block_step(s, it, skip_gain))
    end_state, outs = lax.scan(body_fn, start_state, (xs, bs, cs, steps, logs))
    return (outs.reshape(length, heads, head_size), end_state)


def carry_combine(earlier, later):
    total_e, state_e = earlier
    total_l, state_l = later
    return (total_e + total_l, jnp.exp(total_l)[:, None, None] * state_e + state_l)


def shards(inputs, input_map, output_map, step_raw, step_bias, decay_rate, skip_gain, cotangent):
    length = inputs.shape[1]
    width = inputs.shape[2]
    heads = step_raw.shape[1]
    head_size = width // heads
    states = input_map.shape[2]
    xb = inputs[0].reshape(length, heads, head_size)
    bb = input_map[0]
    cb = output_map[0]
    dyb = cotangent[0].reshape(length, heads, head_size)
    raw = step_raw[0]
    step = jax.nn.softplus(raw + step_bias[:, None])
    logd = -decay_rate[:, None] * step
    cum = jnp.cumsum(logd, axis=1)
    total = cum[:, -1]
    weight_in = jnp.exp(total[:, None] - cum) * step
    scaled_in = (xb.astype(jnp.float32) * weight_in.T[:, :, None]).astype(jnp.bfloat16)
    local_state = jnp.einsum("shp,sn->hpn", scaled_in, bb, preferred_element_type=jnp.float32)
    scaled_grad = dyb.astype(jnp.float32) * jnp.exp(cum).T[:, :, None]
    local_grad = jnp.einsum("thp,tn->hpn", scaled_grad, cb, preferred_element_type=jnp.float32)
    zero_state = jnp.zeros((heads, head_size, states), jnp.float32)
    zero_total = jnp.zeros((heads,), jnp.float32)
    start_state = entering(
        (total, local_state), "seq", carry_combine, (zero_total, zero_state), False
    )[1]
    end_grad = entering((total, local_grad), "seq", carry_combine, (zero_total, zero_state), True)[
        1
    ]

    def local_forward(xv, bv, cv, rv, biasv, ratev, skipv):
        return scan_forward(xv, bv, cv, rv, biasv, ratev, skipv, start_state)

    outputs, pull = jax.vjp(local_forward, xb, bb, cb, raw, step_bias, decay_rate, skip_gain)
    grads = pull((dyb, end_grad))
    params = jnp.stack([grads[4], grads[5], grads[6]])
    total_tokens = length * lax.axis_size("seq") * lax.axis_size("batch")
    summed = lax.psum(params, ("seq", "batch")) * (1.0 / math.sqrt(total_tokens))
    grad_inputs = grads[0].reshape(length, width)[None]
    pair = jnp.stack([summed[0], summed[2]])
    return (
        grad_inputs,
        grads[1].astype(jnp.float32)[None],
        grads[2].astype(jnp.float32)[None],
        grads[3][None],
        pair,
        summed[1],
    )


def solution(mesh):
    in_specs = (
        P("batch", "seq", None),
        P("batch", "seq", None),
        P("batch", "seq", None),
        P("batch", None, "seq"),
        P(),
        P(),
        P(),
        P("batch", "seq", None),
    )
    out_specs = (
        P("batch", "seq", None),
        P("batch", "seq", None),
        P("batch", "seq", None),
        P("batch", None, "seq"),
        P(),
        P(),
    )
    return jax.shard_map(shards, mesh=mesh, in_specs=in_specs, out_specs=out_specs, check_vma=False)
```

profile of v0, /device:TPU:1, one launch (start us, length us, event | category | flops | bytes accessed | tf_op | source)
XLA Modules:
  0.0 635.8 jit_solution(4650788162293645006)
XLA Ops:
  9.6 9.0 %reduce-window.64 = f32[32,8,128]{2,1,0:T(8,128)S(1)} reduce-window(f32[32,8,128]{2,1,0:T(8,128)S(1)} %fusion.79, f32[]{:T(128)} %constant.177.clone.1), window={size=1x1x128 pad=0_0x0_0x127_0}, to_apply=%region_0.1 | reduce-window | flops 4161536 | bytes 262148 | tf_op jit(solution)/shard_map/reduce-window.6
  20.4 6.4 %copy.157 = bf16[1,1024,2048]{1,2,0:T(8,128)(2,1)} copy(bf16[1,1024,2048]{2,1,0:T(8,128)(2,1)} %param.16) | data formatting | bytes 8388608 | tf_op args[0]
  26.8 3.4 fusion.74
  33.4 6.4 %copy.156 = bf16[1,1024,2048]{1,2,0:T(8,128)(2,1)} copy(bf16[1,1024,2048]{2,1,0:T(8,128)(2,1)} %param.23) | data formatting | bytes 8388608 | tf_op args[7]
  39.9 3.4 bitcast_multiply_fusion.5
  43.2 3.2 fusion.77
  46.6 8.0 %reshape_reshape_squeeze.6 = bf16[4,256,32,64]{1,0,3,2:T(4,128)(2,1)} reshape(bf16[1,1024,2048]{1,2,0:T(8,128)(2,1)} %copy.157) | data formatting | bytes 8388608 | tf_op jit(solution)/shard_map/jvp()/reshape;reshape;squeeze | solution.py:60
  54.6 12.9 %reshape.416 = bf16[4,256,32,64]{3,2,1,0:T(8,128)(2,1)} reshape(bf16[1,1024,2048]{2,1,0:T(8,128)(2,1)} %param.23) | data formatting | bytes 8388608 | tf_op jit(solution)/shard_map/transpose(jvp())/reshape;reshape;squeeze | solution.py:67
  69.0 36.4 %all-reduce.2 = f32[512]{0:T(512)S(1)} all-reduce(f32[512]{0:T(512)S(1)} %dynamic-update-slice), channel_id=2, replica_groups=mesh['seq'=16,'batch'=8] {'seq'}, use_global_device_ids=true, to_apply=%add.2 | all-reduce | flops 512 | bytes 4096
  107.1 4.9 copy.160
  112.0 10.4 %copy.167 = bf16[4,256,32,64]{1,3,2,0:T(8,128)(2,1)} copy(bf16[4,256,32,64]{3,2,1,0:T(8,128)(2,1)} %reshape.416) | data formatting | bytes 8388608
  122.4 26.4 %all-gather.8.cloned.1.call-done = f32[512,64,128]{2,1,0:T(8,128)} async-done(((f32[32,64,128]{2,1,0:T(8,128)}), f32[512,64,128]{2,1,0:T(8,128)}) %all-gather.8.cloned.1.call-update) | async-done | bytes 16777232 | tf_op jit(solution)/shard_map/all_gather | solution.py:12
  148.8 24.5 %while.71 = (s32[]{:T(128)}, f32[32,64,128]{2,1,0:T(8,128)S(1)}, s32[]{:T(128)}, f32[16,32]{1,0:T(8,128)S(1)}, f32[16,32,64,128]{3,2,1,0:T(8,128)}, /*index=5*/s32[]{:T(128)}, s32[]{:T(128)}) while((s32[]{:T(128)}, f32[32,64,128]{2,1,0:T(8,128)S(1)}, s32[]{:T(128)}, f32[16,32]{1,0:T(8,128)S(1)}, f32[16,32,64,128]{3,2,1,0:T(8,128)}, ...), condition=%wide.region_5.6_spmd.clone, body=%wide.region_4.5_spmd.clone.sunk | while | flops 1048580 | bytes 3146225 | solution.py:25
  173.3 88.7 %all-gather.6.cloned.1.call-done = f32[512,64,128]{2,1,0:T(8,128)} async-done(((f32[32,64,128]{2,1,0:T(8,128)}), f32[512,64,128]{2,1,0:T(8,128)}) %all-gather.6.cloned.1.call-update) | async-done | bytes 16777232 | tf_op jit(solution)/shard_map/all_gather | solution.py:12
  261.9 24.2 %while.70 = (s32[]{:T(128)}, f32[32,64,128]{2,1,0:T(8,128)S(1)}, s32[]{:T(128)}, f32[16,32]{1,0:T(8,128)S(1)}, f32[16,32,64,128]{3,2,1,0:T(8,128)}, /*index=5*/s32[]{:T(128)}, s32[]{:T(128)}, s32[]{:T(128)}, s32[]{:T(128)}) while((s32[]{:T(128)}, f32[32,64,128]{2,1,0:T(8,128)S(1)}, s32[]{:T(128)}, f32[16,32]{1,0:T(8,128)S(1)}, ...), condition=%wide.region_3.4_spmd.clone, body=%wide.region_2.3_spmd.clone.sunk | while | flops 1048584 | bytes 3146287 | solution.py:25
  286.2 23.5 %while.69 = (s32[]{:T(128)}, f32[32,64,128]{2,1,0:T(8,128)S(1)}, f32[4,32,64,128]{3,2,1,0:T(8,128)}, f32[4,32,256]{2,1,0:T(8,128)}, bf16[4,256,32,64]{1,3,2,0:T(...) while((s32[]{:T(128)}, f32[32,64,128]{2,1,0:T(8,128)S(1)}, ...), condition=%wide.region_9.10_spmd, body=%wide.region_6.9_spmd.sunk | while | flops 137388128 | bytes 5836793 | solution.py:66
  315.0 217.0 %while.72 = (s32[]{:T(128)}, f32[32]{0:T(128)S(1)}, f32[32,64,128]{2,1,0:T(8,128)S(1)}, bf16[4,256,32,64]{1,3,2,0:T(8,128)(2,1)}, bf16[4,256,128]{2,1,0:T(8,128)...) while((s32[]{:T(128)}, f32[32]{0:T(128)S(1)}, ...), condition=%wide.region_24.25_spmd.clone, body=%wide.region_10.0_spmd.clone.sunk | while | flops 1320558848 | bytes 38805324 | solution.py:66
  327.6 8.2 %fusion.164 = (f32[32,256]{1,0:T(8,128)}, f32[32,256]{1,0:T(8,128)}, f32[32,256]{1,0:T(8,128)}, bf16[256,256]{1,0:T(8,128)(2,1)S(1)}) fusion(f32[32,256]{1,0:T(8,128)} %copy.233, f32[32,256]{1,0:T(8,128)} %copy_bitcast_fusion.10, f32[256,256]{1,0:T(8,128)S(1)} %fusion.163, pred[256,256]{1,0:T(8,128)(4,1)} %iota_compare_fusion.2, ...), kind=kOutput, calls=%fused_computation.36.clone.1 | convolution fusion | flops 299802624 | bytes 2719744 | tf_op jit(solution)/shard_map/transpose(jvp())/while/body/eval_jaxpr/checkpoint/hts,shp->thp/dot_general | solution.py:39
  341.9 3.6 fusion.161
  364.6 4.6 fusion.170
  381.9 8.2 %fusion.164 = (f32[32,256]{1,0:T(8,128)}, f32[32,256]{1,0:T(8,128)}, f32[32,256]{1,0:T(8,128)}, bf16[256,256]{1,0:T(8,128)(2,1)S(1)}) fusion(f32[32,256]{1,0:T(8,128)} %copy.233, f32[32,256]{1,0:T(8,128)} %copy_bitcast_fusion.10, f32[256,256]{1,0:T(8,128)S(1)} %fusion.163, pred[256,256]{1,0:T(8,128)(4,1)} %iota_compare_fusion.2, ...), kind=kOutput, calls=%fused_computation.36.clone.1 | convolution fusion | flops 299802624 | bytes 2719744 | tf_op jit(solution)/shard_map/transpose(jvp())/while/body/eval_jaxpr/checkpoint/hts,shp->thp/dot_general | solution.py:39
  396.2 3.6 fusion.161
  418.8 4.6 fusion.170
  436.1 8.2 %fusion.164 = (f32[32,256]{1,0:T(8,128)}, f32[32,256]{1,0:T(8,128)}, f32[32,256]{1,0:T(8,128)}, bf16[256,256]{1,0:T(8,128)(2,1)S(1)}) fusion(f32[32,256]{1,0:T(8,128)} %copy.233, f32[32,256]{1,0:T(8,128)} %copy_bitcast_fusion.10, f32[256,256]{1,0:T(8,128)S(1)} %fusion.163, pred[256,256]{1,0:T(8,128)(4,1)} %iota_compare_fusion.2, ...), kind=kOutput, calls=%fused_computation.36.clone.1 | convolution fusion | flops 299802624 | bytes 2719744 | tf_op jit(solution)/shard_map/transpose(jvp())/while/body/eval_jaxpr/checkpoint/hts,shp->thp/dot_general | solution.py:39
  450.4 3.6 fusion.161
  473.1 4.6 fusion.170
  490.4 8.2 %fusion.164 = (f32[32,256]{1,0:T(8,128)}, f32[32,256]{1,0:T(8,128)}, f32[32,256]{1,0:T(8,128)}, bf16[256,256]{1,0:T(8,128)(2,1)S(1)}) fusion(f32[32,256]{1,0:T(8,128)} %copy.233, f32[32,256]{1,0:T(8,128)} %copy_bitcast_fusion.10, f32[256,256]{1,0:T(8,128)S(1)} %fusion.163, pred[256,256]{1,0:T(8,128)(4,1)} %iota_compare_fusion.2, ...), kind=kOutput, calls=%fused_computation.36.clone.1 | convolution fusion | flops 299802624 | bytes 2719744 | tf_op jit(solution)/shard_map/transpose(jvp())/while/body/eval_jaxpr/checkpoint/hts,shp->thp/dot_general | solution.py:39
  504.7 3.6 fusion.161
  527.3 4.6 fusion.170
  533.9 64.8 %psum.7 = f32[3,32]{1,0:T(4,128)S(1)} all-reduce(f32[3,32]{1,0:T(4,128)S(1)} %pad_maximum_fusion), channel_id=1, replica_groups=mesh['seq'=16,'batch'=8] {'seq','batch'}, use_global_device_ids=true, to_apply=%region_27.28 | all-reduce | flops 96 | bytes 768 | tf_op jit(solution)/shard_map/psum | solution.py:112
  601.2 12.9 %copy.174 = bf16[4,256,32,64]{3,2,1,0:T(8,128)(2,1)} copy(bf16[4,256,32,64]{1,3,2,0:T(8,128)(2,1)} %get-tuple-element.598) | data formatting | bytes 8388608
  614.1 12.4 %reshape.417 = bf16[1,1024,2048]{2,1,0:T(8,128)(2,1)} reshape(bf16[4,256,32,64]{3,2,1,0:T(8,128)(2,1)} %copy.174) | data formatting | bytes 8388608
  (419 shorter events, 244.1 us)
Async XLA Ops:
  7.2 141.7 %all-gather.8.cloned.1.call-start = ((), (), s32[]{:S(2)}) async-start(), calls=%async_computation.1 | async-start | bytes 17825792 | tf_op jit(solution)/shard_map/all_gather | solution.py:12
  7.9 97.6 %copy-start.13 = (f32[32]{0:T(128)}, f32[32]{0:T(128)S(1)}, u32[]{:S(2)}) copy-start(f32[32]{0:T(128)S(1)} %neg.50) | copy-start | bytes 388
  33.4 228.6 %all-gather.6.cloned.1.call-start = ((), (), s32[]{:S(2)}) async-start(), calls=%async_computation | async-start | bytes 17825792 | tf_op jit(solution)/shard_map/all_gather | solution.py:12
  46.6 58.9 %copy-start.7 = (f32[32,4,256]{2,1,0:T(4,128)}, f32[32,4,256]{2,1,0:T(4,128)S(1)}, u32[]{:S(2)}) copy-start(f32[32,4,256]{2,1,0:T(4,128)S(1)} %squeeze.124) | copy-start | bytes 393220
  54.6 12.9 %copy-start.16 = (u32[128]{0:T(128)S(1)}, u32[128]{0:T(128)}, u32[]{:S(2)}) copy-start(u32[128]{0:T(128)} %constant.194) | copy-start | bytes 1540
  54.6 50.9 %copy-start.10 = (f32[32]{0:T(128)S(1)}, f32[32]{0:T(128)}, u32[]{:S(2)}) copy-start(f32[32]{0:T(128)} %param.20) | copy-start | bytes 388
  327.6 8.2 %copy-start.3 = (f32[256,256]{1,0:T(8,128)}, f32[256,256]{1,0:T(8,128)S(1)}, u32[]{:S(2)}) copy-start(f32[256,256]{1,0:T(8,128)S(1)} %fusion.163) | copy-start | bytes 786436 | tf_op jit(solution)/shard_map/transpose(jvp())/while
  345.5 18.4 %copy-start.12 = (f32[32]{0:T(128)S(1)}, f32[32]{0:T(128)}, u32[]{:S(2)}) copy-start(f32[32]{0:T(128)} %fusion.168) | copy-start | bytes 388 | tf_op jit(solution)/shard_map/transpose(jvp())/while
  350.0 7.7 %copy-start.1 = (f32[32,256]{0,1:T(8,128)S(1)}, f32[32,256]{0,1:T(8,128)}, u32[]{:S(2)}) copy-start(f32[32,256]{0,1:T(8,128)} %get-tuple-element.1215) | copy-start | bytes 98308 | tf_op jit(solution)/shard_map/transpose(jvp())/while
  351.0 13.6 %copy-start.4 = (f32[32,256]{1,0:T(8,128)S(1)}, f32[32,256]{1,0:T(8,128)}, u32[]{:S(2)}) copy-start(f32[32,256]{1,0:T(8,128)} %copy_bitcast_fusion.10) | copy-start | bytes 98308 | tf_op jit(solution)/shard_map/transpose(jvp())/while
  351.0 13.6 %copy-start.15 = (f32[32]{0:T(128)S(1)}, f32[32]{0:T(128)}, u32[]{:S(2)}) copy-start(f32[32]{0:T(128)} %get-tuple-element.1211) | copy-start | bytes 388 | tf_op jit(solution)/shard_map/transpose(jvp())/while
  353.0 11.6 %copy-start = (bf16[256,32,64]{0,2,1:T(8,128)(2,1)S(1)}, bf16[256,32,64]{0,2,1:T(8,128)(2,1)}, u32[]{:S(2)}) copy-start(bf16[256,32,64]{0,2,1:T(8,128)(2,1)} %get-tuple-element.1210) | copy-start | bytes 3145732 | tf_op jit(solution)/shard_map/transpose(jvp())/while
  381.9 8.2 %copy-start.3 = (f32[256,256]{1,0:T(8,128)}, f32[256,256]{1,0:T(8,128)S(1)}, u32[]{:S(2)}) copy-start(f32[256,256]{1,0:T(8,128)S(1)} %fusion.163) | copy-start | bytes 786436 | tf_op jit(solution)/shard_map/transpose(jvp())/while
  399.8 18.4 %copy-start.12 = (f32[32]{0:T(128)S(1)}, f32[32]{0:T(128)}, u32[]{:S(2)}) copy-start(f32[32]{0:T(128)} %fusion.168) | copy-start | bytes 388 | tf_op jit(solution)/shard_map/transpose(jvp())/while
  405.2 13.6 %copy-start.4 = (f32[32,256]{1,0:T(8,128)S(1)}, f32[32,256]{1,0:T(8,128)}, u32[]{:S(2)}) copy-start(f32[32,256]{1,0:T(8,128)} %copy_bitcast_fusion.10) | copy-start | bytes 98308 | tf_op jit(solution)/shard_map/transpose(jvp())/while
  405.2 13.6 %copy-start.15 = (f32[32]{0:T(128)S(1)}, f32[32]{0:T(128)}, u32[]{:S(2)}) copy-start(f32[32]{0:T(128)} %get-tuple-element.1211) | copy-start | bytes 388 | tf_op jit(solution)/shard_map/transpose(jvp())/while
  407.2 11.6 %copy-start = (bf16[256,32,64]{0,2,1:T(8,128)(2,1)S(1)}, bf16[256,32,64]{0,2,1:T(8,128)(2,1)}, u32[]{:S(2)}) copy-start(bf16[256,32,64]{0,2,1:T(8,128)(2,1)} %get-tuple-element.1210) | copy-start | bytes 3145732 | tf_op jit(solution)/shard_map/transpose(jvp())/while
  436.1 8.2 %copy-start.3 = (f32[256,256]{1,0:T(8,128)}, f32[256,256]{1,0:T(8,128)S(1)}, u32[]{:S(2)}) copy-start(f32[256,256]{1,0:T(8,128)S(1)} %fusion.163) | copy-start | bytes 786436 | tf_op jit(solution)/shard_map/transpose(jvp())/while
  454.0 18.4 %copy-start.12 = (f32[32]{0:T(128)S(1)}, f32[32]{0:T(128)}, u32[]{:S(2)}) copy-start(f32[32]{0:T(128)} %fusion.168) | copy-start | bytes 388 | tf_op jit(solution)/shard_map/transpose(jvp())/while
  459.5 13.6 %copy-start.4 = (f32[32,256]{1,0:T(8,128)S(1)}, f32[32,256]{1,0:T(8,128)}, u32[]{:S(2)}) copy-start(f32[32,256]{1,0:T(8,128)} %copy_bitcast_fusion.10) | copy-start | bytes 98308 | tf_op jit(solution)/shard_map/transpose(jvp())/while
  459.5 13.6 %copy-start.15 = (f32[32]{0:T(128)S(1)}, f32[32]{0:T(128)}, u32[]{:S(2)}) copy-start(f32[32]{0:T(128)} %get-tuple-element.1211) | copy-start | bytes 388 | tf_op jit(solution)/shard_map/transpose(jvp())/while
  461.5 11.6 %copy-start = (bf16[256,32,64]{0,2,1:T(8,128)(2,1)S(1)}, bf16[256,32,64]{0,2,1:T(8,128)(2,1)}, u32[]{:S(2)}) copy-start(bf16[256,32,64]{0,2,1:T(8,128)(2,1)} %get-tuple-element.1210) | copy-start | bytes 3145732 | tf_op jit(solution)/shard_map/transpose(jvp())/while
  490.4 8.2 %copy-start.3 = (f32[256,256]{1,0:T(8,128)}, f32[256,256]{1,0:T(8,128)S(1)}, u32[]{:S(2)}) copy-start(f32[256,256]{1,0:T(8,128)S(1)} %fusion.163) | copy-start | bytes 786436 | tf_op jit(solution)/shard_map/transpose(jvp())/while
  508.2 18.4 %copy-start.12 = (f32[32]{0:T(128)S(1)}, f32[32]{0:T(128)}, u32[]{:S(2)}) copy-start(f32[32]{0:T(128)} %fusion.168) | copy-start | bytes 388 | tf_op jit(solution)/shard_map/transpose(jvp())/while
  513.7 13.6 %copy-start.4 = (f32[32,256]{1,0:T(8,128)S(1)}, f32[32,256]{1,0:T(8,128)}, u32[]{:S(2)}) copy-start(f32[32,256]{1,0:T(8,128)} %copy_bitcast_fusion.10) | copy-start | bytes 98308 | tf_op jit(solution)/shard_map/transpose(jvp())/while
  513.7 13.6 %copy-start.15 = (f32[32]{0:T(128)S(1)}, f32[32]{0:T(128)}, u32[]{:S(2)}) copy-start(f32[32]{0:T(128)} %get-tuple-element.1211) | copy-start | bytes 388 | tf_op jit(solution)/shard_map/transpose(jvp())/while
  515.7 11.6 %copy-start = (bf16[256,32,64]{0,2,1:T(8,128)(2,1)S(1)}, bf16[256,32,64]{0,2,1:T(8,128)(2,1)}, u32[]{:S(2)}) copy-start(bf16[256,32,64]{0,2,1:T(8,128)(2,1)} %get-tuple-element.1210) | copy-start | bytes 3145732 | tf_op jit(solution)/shard_map/transpose(jvp())/while
  614.1 13.0 %copy-start.6 = (f32[1,32,1024]{2,1,0:T(8,128)S(1)}, f32[1,32,1024]{2,1,0:T(8,128)}, u32[]{:S(2)}) copy-start(f32[1,32,1024]{2,1,0:T(8,128)} %param.19) | copy-start | bytes 393220
  614.1 13.0 %copy-start.11 = (f32[32]{0:T(128)S(1)}, f32[32]{0:T(128)}, u32[]{:S(2)}) copy-start(f32[32]{0:T(128)} %param.20) | copy-start | bytes 388
  614.1 13.0 %copy-start.14 = (f32[32]{0:T(128)S(1)}, f32[32]{0:T(128)}, u32[]{:S(2)}) copy-start(f32[32]{0:T(128)} %copy-done.13) | copy-start | bytes 388
  614.1 13.8 %copy-start.8 = (bf16[4,256,128]{2,1,0:T(8,128)(2,1)S(1)}, bf16[4,256,128]{2,1,0:T(8,128)(2,1)}, u32[]{:S(2)}) copy-start(bf16[4,256,128]{2,1,0:T(8,128)(2,1)} %get-tuple-element.600) | copy-start | bytes 786436
  614.1 13.8 %copy-start.9 = (bf16[4,256,128]{2,1,0:T(8,128)(2,1)S(1)}, bf16[4,256,128]{2,1,0:T(8,128)(2,1)}, u32[]{:S(2)}) copy-start(bf16[4,256,128]{2,1,0:T(8,128)(2,1)} %get-tuple-element.599) | copy-start | bytes 786436
  (8 other events, 54.7 us)
Sparse Core Ops, SparseCore 0:
  33.5 115.2 all-gather.7
  151.0 110.9 all-gather.5
where the time goes:
time: 643 us; the launch traced here: 636 us
  local copies, waits for them, and re-layouts  189 us (29%)
  waiting for transfers between devices  115 us (18%)
  matrix products  108 us (17%)
  other arithmetic  106 us (16%)
  blocking collectives  101 us (16%)
  between operations  14.9 us (2%)
    all_gather x2, waiting for transfers between devices, entering(): everything = jax.tree.map(lambda part: lax.all_gather(part, axis), array)  115 us
    psum x1, blocking collectives, shards(): lax.psum(params, ('seq', 'batch')) * (1.0 / math.sqrt(total_tokens))  64.8 us
    dot_general x8, matrix products, block_step(): jnp.einsum('hts,shp->thp', weights, xc, preferred_element_type=jnp.float32)  51.3 us
    unnamed x30, local copies, waits for them, and re-layouts  50.4 us
    select_n x32, other arithmetic, lap(): return jax.tree.map(lambda a, b: jnp.where(reached, a, b), new, before)  47.2 us
    unnamed x1, blocking collectives  36.4 us
    dot_general x12, matrix products, block_step(): jnp.einsum('shp,sn->hpn', scaled, bc, preferred_element_type=jnp.float32)  31.1 us
    another operation x39, other arithmetic  27.7 us
  transfers between devices with their start and end apart: 2, of which 2 were waited for; matrix products, arithmetic and copies ran while one was open for 12% of the time, Pallas kernels for 0%

commit v1 on v0

--- a/solution.py
+++ b/solution.py
@@ -109,7 +109,9 @@
     grads = pull((dyb, end_grad))
     params = jnp.stack([grads[4], grads[5], grads[6]])
     total_tokens = length * lax.axis_size("seq") * lax.axis_size("batch")
-    summed = lax.psum(params, ("seq", "batch")) * (1.0 / math.sqrt(total_tokens))
+    summed = jnp.sum(lax.all_gather(params, ("seq", "batch")), axis=0) * (
+        1.0 / math.sqrt(total_tokens)
+    )
     grad_inputs = grads[0].reshape(length, width)[None]
     pair = jnp.stack([summed[0], summed[2]])
     return (

time: 643 us -> 614 us (0.955)
  blocking collectives: 101 us -> 72.4 us
    psum x1 -> x0, blocking collectives: 64.8 us -> none  [shards(): lax.psum(params, ('seq', 'batch')) * (1.0 / math.sqrt(total_tokens))]
    all_gather x0 -> x1, blocking collectives: none -> 36 us  [shards(): lax.all_gather(params, ('seq', 'batch'))]
    another operation x40 -> x39, other arithmetic: 27.7 us -> 27.7 us
where the time goes in v1:
time: 614 us; the launch traced here: 607 us
  local copies, waits for them, and re-layouts  189 us (31%)
  waiting for transfers between devices  115 us (19%)
  matrix products  108 us (18%)
  other arithmetic  106 us (17%)
  blocking collectives  72.4 us (12%)
  between operations  14.9 us (2%)
    all_gather x2, waiting for transfers between devices, entering(): everything = jax.tree.map(lambda part: lax.all_gather(part, axis), array)  115 us
    dot_general x8, matrix products, block_step(): jnp.einsum('hts,shp->thp', weights, xc, preferred_element_type=jnp.float32)  51.3 us
    unnamed x30, local copies, waits for them, and re-layouts  50.4 us
    select_n x32, other arithmetic, lap(): return jax.tree.map(lambda a, b: jnp.where(reached, a, b), new, before)  47.2 us
    unnamed x1, blocking collectives  36.4 us
    all_gather x1, blocking collectives, shards(): lax.all_gather(params, ('seq', 'batch'))  36 us
    dot_general x12, matrix products, block_step(): jnp.einsum('shp,sn->hpn', scaled, bc, preferred_element_type=jnp.float32)  31.1 us
    another operation x39, other arithmetic  27.7 us
  transfers between devices with their start and end apart: 2, of which 2 were waited for; matrix products, arithmetic and copies ran while one was open for 12% of the time, Pallas kernels for 0%

profile of v1, /device:TPU:1, one launch (start us, length us, event | category | flops | bytes accessed | tf_op | source)
XLA Modules:
  0.0 607.2 jit_solution(7455594441476788650)
XLA Ops:
  9.6 9.0 %reduce-window.64 = f32[32,8,128]{2,1,0:T(8,128)S(1)} reduce-window(f32[32,8,128]{2,1,0:T(8,128)S(1)} %fusion.79, f32[]{:T(128)} %constant.177.clone.1), window={size=1x1x128 pad=0_0x0_0x127_0}, to_apply=%region_0.1 | reduce-window | flops 4161536 | bytes 262148 | tf_op jit(solution)/shard_map/reduce-window.6
  20.4 6.4 %copy.157 = bf16[1,1024,2048]{1,2,0:T(8,128)(2,1)} copy(bf16[1,1024,2048]{2,1,0:T(8,128)(2,1)} %param.16) | data formatting | bytes 8388608 | tf_op args[0]
  26.8 3.4 fusion.74
  33.4 6.4 %copy.156 = bf16[1,1024,2048]{1,2,0:T(8,128)(2,1)} copy(bf16[1,1024,2048]{2,1,0:T(8,128)(2,1)} %param.23) | data formatting | bytes 8388608 | tf_op args[7]
  39.9 3.4 bitcast_multiply_fusion.5
  43.2 3.2 fusion.77
  46.6 8.0 %reshape_reshape_squeeze.6 = bf16[4,256,32,64]{1,0,3,2:T(4,128)(2,1)} reshape(bf16[1,1024,2048]{1,2,0:T(8,128)(2,1)} %copy.157) | data formatting | bytes 8388608 | tf_op jit(solution)/shard_map/jvp()/reshape;reshape;squeeze | solution.py:60
  54.6 12.9 %reshape.420 = bf16[4,256,32,64]{3,2,1,0:T(8,128)(2,1)} reshape(bf16[1,1024,2048]{2,1,0:T(8,128)(2,1)} %param.23) | data formatting | bytes 8388608 | tf_op jit(solution)/shard_map/transpose(jvp())/reshape;reshape;squeeze | solution.py:67
  69.0 36.4 %all-reduce.2 = f32[512]{0:T(512)S(1)} all-reduce(f32[512]{0:T(512)S(1)} %dynamic-update-slice), channel_id=2, replica_groups=mesh['seq'=16,'batch'=8] {'seq'}, use_global_device_ids=true, to_apply=%add.2 | all-reduce | flops 512 | bytes 4096
  107.1 4.9 copy.160
  112.0 10.4 %copy.167 = bf16[4,256,32,64]{1,3,2,0:T(8,128)(2,1)} copy(bf16[4,256,32,64]{3,2,1,0:T(8,128)(2,1)} %reshape.420) | data formatting | bytes 8388608
  122.4 26.4 %all-gather.10.cloned.1.call-done = f32[512,64,128]{2,1,0:T(8,128)} async-done(((f32[32,64,128]{2,1,0:T(8,128)}), f32[512,64,128]{2,1,0:T(8,128)}) %all-gather.10.cloned.1.call-update) | async-done | bytes 16777232 | tf_op jit(solution)/shard_map/all_gather | solution.py:12
  148.8 24.5 %while.71 = (s32[]{:T(128)}, f32[32,64,128]{2,1,0:T(8,128)S(1)}, s32[]{:T(128)}, f32[16,32]{1,0:T(8,128)S(1)}, f32[16,32,64,128]{3,2,1,0:T(8,128)}, /*index=5*/s32[]{:T(128)}, s32[]{:T(128)}) while((s32[]{:T(128)}, f32[32,64,128]{2,1,0:T(8,128)S(1)}, s32[]{:T(128)}, f32[16,32]{1,0:T(8,128)S(1)}, f32[16,32,64,128]{3,2,1,0:T(8,128)}, ...), condition=%wide.region_5.6_spmd.clone, body=%wide.region_4.5_spmd.clone.sunk | while | flops 1048580 | bytes 3146225 | solution.py:25
  173.3 88.7 %all-gather.8.cloned.1.call-done = f32[512,64,128]{2,1,0:T(8,128)} async-done(((f32[32,64,128]{2,1,0:T(8,128)}), f32[512,64,128]{2,1,0:T(8,128)}) %all-gather.8.cloned.1.call-update) | async-done | bytes 16777232 | tf_op jit(solution)/shard_map/all_gather | solution.py:12
  261.9 24.2 %while.70 = (s32[]{:T(128)}, f32[32,64,128]{2,1,0:T(8,128)S(1)}, s32[]{:T(128)}, f32[16,32]{1,0:T(8,128)S(1)}, f32[16,32,64,128]{3,2,1,0:T(8,128)}, /*index=5*/s32[]{:T(128)}, s32[]{:T(128)}, s32[]{:T(128)}, s32[]{:T(128)}) while((s32[]{:T(128)}, f32[32,64,128]{2,1,0:T(8,128)S(1)}, s32[]{:T(128)}, f32[16,32]{1,0:T(8,128)S(1)}, ...), condition=%wide.region_3.4_spmd.clone, body=%wide.region_2.3_spmd.clone.sunk | while | flops 1048584 | bytes 3146287 | solution.py:25
  286.2 23.5 %while.69 = (s32[]{:T(128)}, f32[32,64,128]{2,1,0:T(8,128)S(1)}, f32[4,32,64,128]{3,2,1,0:T(8,128)}, f32[4,32,256]{2,1,0:T(8,128)}, bf16[4,256,32,64]{1,3,2,0:T(...) while((s32[]{:T(128)}, f32[32,64,128]{2,1,0:T(8,128)S(1)}, ...), condition=%wide.region_9.10_spmd, body=%wide.region_6.9_spmd.sunk | while | flops 137388128 | bytes 5836793 | solution.py:66
  315.0 217.0 %while.72 = (s32[]{:T(128)}, f32[32]{0:T(128)S(1)}, f32[32,64,128]{2,1,0:T(8,128)S(1)}, bf16[4,256,32,64]{1,3,2,0:T(8,128)(2,1)}, bf16[4,256,128]{2,1,0:T(8,128)...) while((s32[]{:T(128)}, f32[32]{0:T(128)S(1)}, ...), condition=%wide.region_24.25_spmd.clone, body=%wide.region_10.0_spmd.clone.sunk | while | flops 1320558848 | bytes 38805324 | solution.py:66
  327.6 8.2 %fusion.164 = (f32[32,256]{1,0:T(8,128)}, f32[32,256]{1,0:T(8,128)}, f32[32,256]{1,0:T(8,128)}, bf16[256,256]{1,0:T(8,128)(2,1)S(1)}) fusion(f32[32,256]{1,0:T(8,128)} %copy.234, f32[32,256]{1,0:T(8,128)} %copy_bitcast_fusion.10, f32[256,256]{1,0:T(8,128)S(1)} %fusion.163, pred[256,256]{1,0:T(8,128)(4,1)} %iota_compare_fusion.2, ...), kind=kOutput, calls=%fused_computation.36.clone.1 | convolution fusion | flops 299802624 | bytes 2719744 | tf_op jit(solution)/shard_map/transpose(jvp())/while/body/eval_jaxpr/checkpoint/hts,shp->thp/dot_general | solution.py:39
  341.9 3.6 fusion.161
  364.6 4.6 fusion.170
  381.9 8.2 %fusion.164 = (f32[32,256]{1,0:T(8,128)}, f32[32,256]{1,0:T(8,128)}, f32[32,256]{1,0:T(8,128)}, bf16[256,256]{1,0:T(8,128)(2,1)S(1)}) fusion(f32[32,256]{1,0:T(8,128)} %copy.234, f32[32,256]{1,0:T(8,128)} %copy_bitcast_fusion.10, f32[256,256]{1,0:T(8,128)S(1)} %fusion.163, pred[256,256]{1,0:T(8,128)(4,1)} %iota_compare_fusion.2, ...), kind=kOutput, calls=%fused_computation.36.clone.1 | convolution fusion | flops 299802624 | bytes 2719744 | tf_op jit(solution)/shard_map/transpose(jvp())/while/body/eval_jaxpr/checkpoint/hts,shp->thp/dot_general | solution.py:39
  396.2 3.6 fusion.161
  418.8 4.6 fusion.170
  436.1 8.2 %fusion.164 = (f32[32,256]{1,0:T(8,128)}, f32[32,256]{1,0:T(8,128)}, f32[32,256]{1,0:T(8,128)}, bf16[256,256]{1,0:T(8,128)(2,1)S(1)}) fusion(f32[32,256]{1,0:T(8,128)} %copy.234, f32[32,256]{1,0:T(8,128)} %copy_bitcast_fusion.10, f32[256,256]{1,0:T(8,128)S(1)} %fusion.163, pred[256,256]{1,0:T(8,128)(4,1)} %iota_compare_fusion.2, ...), kind=kOutput, calls=%fused_computation.36.clone.1 | convolution fusion | flops 299802624 | bytes 2719744 | tf_op jit(solution)/shard_map/transpose(jvp())/while/body/eval_jaxpr/checkpoint/hts,shp->thp/dot_general | solution.py:39
  450.4 3.6 fusion.161
  473.1 4.6 fusion.170
  490.4 8.2 %fusion.164 = (f32[32,256]{1,0:T(8,128)}, f32[32,256]{1,0:T(8,128)}, f32[32,256]{1,0:T(8,128)}, bf16[256,256]{1,0:T(8,128)(2,1)S(1)}) fusion(f32[32,256]{1,0:T(8,128)} %copy.234, f32[32,256]{1,0:T(8,128)} %copy_bitcast_fusion.10, f32[256,256]{1,0:T(8,128)S(1)} %fusion.163, pred[256,256]{1,0:T(8,128)(4,1)} %iota_compare_fusion.2, ...), kind=kOutput, calls=%fused_computation.36.clone.1 | convolution fusion | flops 299802624 | bytes 2719744 | tf_op jit(solution)/shard_map/transpose(jvp())/while/body/eval_jaxpr/checkpoint/hts,shp->thp/dot_general | solution.py:39
  504.7 3.6 fusion.161
  527.3 4.6 fusion.170
  535.8 36.0 %all-gather.4 = f32[128,3,32]{2,1,0:T(4,128)S(1)} all-gather(f32[1,3,32]{2,1,0:T(4,128)S(1)} %maximum_bitcast_fusion), channel_id=5, replica_groups=mesh['seq'=16,'batch'=8] {'seq','batch'}, dimensions={0}, use_global_device_ids=true | all-gather | bytes 49536 | tf_op jit(solution)/shard_map/all_gather | solution.py:112
  572.5 12.9 %copy.174 = bf16[4,256,32,64]{3,2,1,0:T(8,128)(2,1)} copy(bf16[4,256,32,64]{1,3,2,0:T(8,128)(2,1)} %get-tuple-element.598) | data formatting | bytes 8388608
  585.5 12.4 %reshape.421 = bf16[1,1024,2048]{2,1,0:T(8,128)(2,1)} reshape(bf16[4,256,32,64]{3,2,1,0:T(8,128)(2,1)} %copy.174) | data formatting | bytes 8388608
  (420 shorter events, 244.2 us)
Async XLA Ops:
  7.2 141.7 %all-gather.10.cloned.1.call-start = ((), (), s32[]{:S(2)}) async-start(), calls=%async_computation.1 | async-start | bytes 17825792 | tf_op jit(solution)/shard_map/all_gather | solution.py:12
  7.9 97.6 %copy-start.13 = (f32[32]{0:T(128)}, f32[32]{0:T(128)S(1)}, u32[]{:S(2)}) copy-start(f32[32]{0:T(128)S(1)} %neg.50) | copy-start | bytes 388
  33.4 228.6 %all-gather.8.cloned.1.call-start = ((), (), s32[]{:S(2)}) async-start(), calls=%async_computation | async-start | bytes 17825792 | tf_op jit(solution)/shard_map/all_gather | solution.py:12
  46.6 58.9 %copy-start.7 = (f32[32,4,256]{2,1,0:T(4,128)}, f32[32,4,256]{2,1,0:T(4,128)S(1)}, u32[]{:S(2)}) copy-start(f32[32,4,256]{2,1,0:T(4,128)S(1)} %squeeze.124) | copy-start | bytes 393220
  54.6 12.9 %copy-start.16 = (u32[128]{0:T(128)S(1)}, u32[128]{0:T(128)}, u32[]{:S(2)}) copy-start(u32[128]{0:T(128)} %constant.194) | copy-start | bytes 1540
  54.6 50.9 %copy-start.10 = (f32[32]{0:T(128)S(1)}, f32[32]{0:T(128)}, u32[]{:S(2)}) copy-start(f32[32]{0:T(128)} %param.20) | copy-start | bytes 388
  327.6 8.2 %copy-start.3 = (f32[256,256]{1,0:T(8,128)}, f32[256,256]{1,0:T(8,128)S(1)}, u32[]{:S(2)}) copy-start(f32[256,256]{1,0:T(8,128)S(1)} %fusion.163) | copy-start | bytes 786436 | tf_op jit(solution)/shard_map/transpose(jvp())/while
  345.5 18.4 %copy-start.12 = (f32[32]{0:T(128)S(1)}, f32[32]{0:T(128)}, u32[]{:S(2)}) copy-start(f32[32]{0:T(128)} %fusion.168) | copy-start | bytes 388 | tf_op jit(solution)/shard_map/transpose(jvp())/while
  350.0 7.7 %copy-start.1 = (f32[32,256]{0,1:T(8,128)S(1)}, f32[32,256]{0,1:T(8,128)}, u32[]{:S(2)}) copy-start(f32[32,256]{0,1:T(8,128)} %get-tuple-element.1215) | copy-start | bytes 98308 | tf_op jit(solution)/shard_map/transpose(jvp())/while
  351.0 13.6 %copy-start.4 = (f32[32,256]{1,0:T(8,128)S(1)}, f32[32,256]{1,0:T(8,128)}, u32[]{:S(2)}) copy-start(f32[32,256]{1,0:T(8,128)} %copy_bitcast_fusion.10) | copy-start | bytes 98308 | tf_op jit(solution)/shard_map/transpose(jvp())/while
  351.0 13.6 %copy-start.15 = (f32[32]{0:T(128)S(1)}, f32[32]{0:T(128)}, u32[]{:S(2)}) copy-start(f32[32]{0:T(128)} %get-tuple-element.1211) | copy-start | bytes 388 | tf_op jit(solution)/shard_map/transpose(jvp())/while
  353.0 11.6 %copy-start = (bf16[256,32,64]{0,2,1:T(8,128)(2,1)S(1)}, bf16[256,32,64]{0,2,1:T(8,128)(2,1)}, u32[]{:S(2)}) copy-start(bf16[256,32,64]{0,2,1:T(8,128)(2,1)} %get-tuple-element.1210) | copy-start | bytes 3145732 | tf_op jit(solution)/shard_map/transpose(jvp())/while
  381.9 8.2 %copy-start.3 = (f32[256,256]{1,0:T(8,128)}, f32[256,256]{1,0:T(8,128)S(1)}, u32[]{:S(2)}) copy-start(f32[256,256]{1,0:T(8,128)S(1)} %fusion.163) | copy-start | bytes 786436 | tf_op jit(solution)/shard_map/transpose(jvp())/while
  399.8 18.4 %copy-start.12 = (f32[32]{0:T(128)S(1)}, f32[32]{0:T(128)}, u32[]{:S(2)}) copy-start(f32[32]{0:T(128)} %fusion.168) | copy-start | bytes 388 | tf_op jit(solution)/shard_map/transpose(jvp())/while
  405.2 13.6 %copy-start.4 = (f32[32,256]{1,0:T(8,128)S(1)}, f32[32,256]{1,0:T(8,128)}, u32[]{:S(2)}) copy-start(f32[32,256]{1,0:T(8,128)} %copy_bitcast_fusion.10) | copy-start | bytes 98308 | tf_op jit(solution)/shard_map/transpose(jvp())/while
  405.2 13.6 %copy-start.15 = (f32[32]{0:T(128)S(1)}, f32[32]{0:T(128)}, u32[]{:S(2)}) copy-start(f32[32]{0:T(128)} %get-tuple-element.1211) | copy-start | bytes 388 | tf_op jit(solution)/shard_map/transpose(jvp())/while
  407.2 11.6 %copy-start = (bf16[256,32,64]{0,2,1:T(8,128)(2,1)S(1)}, bf16[256,32,64]{0,2,1:T(8,128)(2,1)}, u32[]{:S(2)}) copy-start(bf16[256,32,64]{0,2,1:T(8,128)(2,1)} %get-tuple-element.1210) | copy-start | bytes 3145732 | tf_op jit(solution)/shard_map/transpose(jvp())/while
  436.1 8.2 %copy-start.3 = (f32[256,256]{1,0:T(8,128)}, f32[256,256]{1,0:T(8,128)S(1)}, u32[]{:S(2)}) copy-start(f32[256,256]{1,0:T(8,128)S(1)} %fusion.163) | copy-start | bytes 786436 | tf_op jit(solution)/shard_map/transpose(jvp())/while
  454.0 18.4 %copy-start.12 = (f32[32]{0:T(128)S(1)}, f32[32]{0:T(128)}, u32[]{:S(2)}) copy-start(f32[32]{0:T(128)} %fusion.168) | copy-start | bytes 388 | tf_op jit(solution)/shard_map/transpose(jvp())/while
  459.5 13.6 %copy-start.4 = (f32[32,256]{1,0:T(8,128)S(1)}, f32[32,256]{1,0:T(8,128)}, u32[]{:S(2)}) copy-start(f32[32,256]{1,0:T(8,128)} %copy_bitcast_fusion.10) | copy-start | bytes 98308 | tf_op jit(solution)/shard_map/transpose(jvp())/while
  459.5 13.6 %copy-start.15 = (f32[32]{0:T(128)S(1)}, f32[32]{0:T(128)}, u32[]{:S(2)}) copy-start(f32[32]{0:T(128)} %get-tuple-element.1211) | copy-start | bytes 388 | tf_op jit(solution)/shard_map/transpose(jvp())/while
  461.5 11.6 %copy-start = (bf16[256,32,64]{0,2,1:T(8,128)(2,1)S(1)}, bf16[256,32,64]{0,2,1:T(8,128)(2,1)}, u32[]{:S(2)}) copy-start(bf16[256,32,64]{0,2,1:T(8,128)(2,1)} %get-tuple-element.1210) | copy-start | bytes 3145732 | tf_op jit(solution)/shard_map/transpose(jvp())/while
  490.4 8.2 %copy-start.3 = (f32[256,256]{1,0:T(8,128)}, f32[256,256]{1,0:T(8,128)S(1)}, u32[]{:S(2)}) copy-start(f32[256,256]{1,0:T(8,128)S(1)} %fusion.163) | copy-start | bytes 786436 | tf_op jit(solution)/shard_map/transpose(jvp())/while
  508.2 18.4 %copy-start.12 = (f32[32]{0:T(128)S(1)}, f32[32]{0:T(128)}, u32[]{:S(2)}) copy-start(f32[32]{0:T(128)} %fusion.168) | copy-start | bytes 388 | tf_op jit(solution)/shard_map/transpose(jvp())/while
  513.7 13.6 %copy-start.4 = (f32[32,256]{1,0:T(8,128)S(1)}, f32[32,256]{1,0:T(8,128)}, u32[]{:S(2)}) copy-start(f32[32,256]{1,0:T(8,128)} %copy_bitcast_fusion.10) | copy-start | bytes 98308 | tf_op jit(solution)/shard_map/transpose(jvp())/while
  513.7 13.6 %copy-start.15 = (f32[32]{0:T(128)S(1)}, f32[32]{0:T(128)}, u32[]{:S(2)}) copy-start(f32[32]{0:T(128)} %get-tuple-element.1211) | copy-start | bytes 388 | tf_op jit(solution)/shard_map/transpose(jvp())/while
  515.7 11.6 %copy-start = (bf16[256,32,64]{0,2,1:T(8,128)(2,1)S(1)}, bf16[256,32,64]{0,2,1:T(8,128)(2,1)}, u32[]{:S(2)}) copy-start(bf16[256,32,64]{0,2,1:T(8,128)(2,1)} %get-tuple-element.1210) | copy-start | bytes 3145732 | tf_op jit(solution)/shard_map/transpose(jvp())/while
  585.5 12.4 %copy-start.6 = (f32[1,32,1024]{2,1,0:T(8,128)S(1)}, f32[1,32,1024]{2,1,0:T(8,128)}, u32[]{:S(2)}) copy-start(f32[1,32,1024]{2,1,0:T(8,128)} %param.19) | copy-start | bytes 393220
  585.5 12.4 %copy-start.11 = (f32[32]{0:T(128)S(1)}, f32[32]{0:T(128)}, u32[]{:S(2)}) copy-start(f32[32]{0:T(128)} %param.20) | copy-start | bytes 388
  585.5 12.4 %copy-start.14 = (f32[32]{0:T(128)S(1)}, f32[32]{0:T(128)}, u32[]{:S(2)}) copy-start(f32[32]{0:T(128)} %copy-done.13) | copy-start | bytes 388
  585.5 13.9 %copy-start.8 = (bf16[4,256,128]{2,1,0:T(8,128)(2,1)S(1)}, bf16[4,256,128]{2,1,0:T(8,128)(2,1)}, u32[]{:S(2)}) copy-start(bf16[4,256,128]{2,1,0:T(8,128)(2,1)} %get-tuple-element.600) | copy-start | bytes 786436
  585.5 13.8 %copy-start.9 = (bf16[4,256,128]{2,1,0:T(8,128)(2,1)S(1)}, bf16[4,256,128]{2,1,0:T(8,128)(2,1)}, u32[]{:S(2)}) copy-start(bf16[4,256,128]{2,1,0:T(8,128)(2,1)} %get-tuple-element.599) | copy-start | bytes 786436
  (8 other events, 54.7 us)
Sparse Core Ops, SparseCore 0:
  33.5 115.2 all-gather.9
  151.0 110.9 all-gather.7
